TPU v7x, 32 devices: a whole 2x2x4 slice. The times are simulated.
32 devices in a mesh: tx: 4 (over z), ty: 8 (over y, x, core).
Axes of the slice: x: 2, y: 2, z: 4, core: 2. Of those that a mesh axis runs over, the one named last changes fastest.
Arguments:
- source: bfloat16 [256, 512, 2, 128], P('tx', 'ty'), may hold values from -6 to 6
- guess: bfloat16 [256, 512, 2, 128], P('tx', 'ty'), may hold values from -6 to 6
- coefficient: float32 [256, 512], P('tx', 'ty'), may hold values from 0.25 to 2.5
- leaf_map: float32 [4, 8, 2, 256, 256], P('tx', 'ty'), may hold values from -0.9 to 0.9, as said below
- body_map: bfloat16 [4, 8, 2, 256, 4096], P('tx', 'ty'), may hold values from -0.013671875 to 0.013671875
Outputs:
- top_map: float32 [4, 8, 2, 64, 768], P('tx', 'ty')
- top_outgoing: float32 [4, 8, 2, 64, 128], P('tx', 'ty')
Inputs may be any that keep to these rules, and one draw needn't show every extreme that they name: `leaf_map`: as a complex matrix, each tile's map has spectral norm at most 0.9.
All inputs are finite; a program needn't handle non-finite values.
Results may differ from a plain program's by a relative error of at most 0.0029.
Values may be sent and summed in bfloat16 or wider, within the bound.
A program may use at most 64 MiB of HBM per device.

v0:
```python
import functools

import jax
import jax.numpy as jnp
from jax import lax
from jax.experimental import pallas as pl
from jax.experimental.pallas import tpu as pltpu
from jax.sharding import PartitionSpec as P

DAMPING = 0.5
DOUBLINGS = 7
LANES = 128
MESH = pl.DeviceIdType.MESH
F32 = jnp.float32
BF16 = jnp.bfloat16


def split(x):
    high = x.astype(BF16)
    return high, (x - high.astype(F32)).astype(BF16)


def dot1(a, b):
    return jnp.dot(a, b, preferred_element_type=F32)


def dot3(a, b):
    a_high, a_low = split(a)
    b_high, b_low = split(b)
    return dot1(a_high, b_high) + (dot1(a_high, b_low) + dot1(a_low, b_high))


def tile(x, k):
    return x[:, k * LANES : (k + 1) * LANES]


def cols(parts):
    return jnp.concatenate(parts, axis=1)


def rows(parts):
    return jnp.concatenate(parts, axis=0)


def half_roll(x):
    return pltpu.roll(x, LANES // 2, 1)


def low_lanes(shape):
    return lax.broadcasted_iota(jnp.int32, shape, 1) < LANES // 2


def low_low(a, b):
    return jnp.where(low_lanes(a.shape), a, half_roll(b))


def high_high(a, b):
    return jnp.where(low_lanes(a.shape), half_roll(a), b)


def embed(re, im):
    return rows([cols([re, -im]), cols([im, re])])


def embed_low(re, im):
    return rows([low_low(re, -im), low_low(im, re)])


def identity(n):
    return (
        lax.broadcasted_iota(jnp.int32, (n, n), 0) == lax.broadcasted_iota(jnp.int32, (n, n), 1)
    ).astype(F32)


def inverse(power, pow_ref, inv_ref):
    n = power.shape[0]
    pow_ref[:n, :n] = dot3(power, power)
    inv_ref[:n, :n] = identity(n) + power

    def body(k, carry):
        now, total = pow_ref[:n, :n], inv_ref[:n, :n]
        both = dot3(now, cols([now, total]))
        pow_ref[:n, :n] = both[:, :n]
        inv_ref[:n, :n] = total + both[:, n:]
        return carry

    lax.fori_loop(0, DOUBLINGS - 2, body, 0)
    total = inv_ref[:n, :n]
    return total + dot3(pow_ref[:n, :n], total)


def swapped_view(block):
    return cols([half_roll(tile(block, 0)), tile(block, 2), tile(block, 1), tile(block, 3)])


def merge_kernel(
    map_ref, out_ref, top_ref, top_out_ref,
    own0, face1, face2, x1, x2, face3, pow_ref, inv_ref,
    send1, recv1, send2, recv2, send3, recv3,
):
    p = lax.axis_index("tx")
    q = lax.axis_index("ty")
    p_low = lax.rem(p, 4)
    p_odd = lax.rem(p, 2)
    q_odd = lax.rem(q, 2)
    vertical = p + 1 - 2 * p_odd
    beside = q + 1 - 2 * q_odd
    inner = (p_low == 1) | (p_low == 2)
    inner_num = jnp.where(inner, 1, 0)
    lower = p_low < 2
    facing = p + 3 - 2 * p_low
    side = map_ref.shape[1] // 4

    barrier = pltpu.get_barrier_semaphore()
    for target in ((vertical, q), (p, beside)):
        pl.semaphore_signal(barrier, inc=1, device_id=target, device_id_type=MESH)

    @pl.when(inner)
    def _():
        pl.semaphore_signal(barrier, inc=1, device_id=(facing, q), device_id_type=MESH)

    pl.semaphore_wait(barrier, 2 + inner_num)

    def remote(src, dst, send, recv, target):
        return pltpu.make_async_remote_copy(
            src_ref=src, dst_ref=dst, send_sem=send, recv_sem=recv,
            device_id=target, device_id_type=MESH,
        )

    starts = [
        jnp.where(p_odd == 1, 0, 2 * side),
        jnp.where(q_odd == 1, 3 * side, side),
        jnp.where(p_odd == 1, 2 * side, 0),
        jnp.where(q_odd == 1, side, 3 * side),
    ]
    lane = lax.broadcasted_iota(jnp.int32, (side, LANES), 1)
    vert_swap = jnp.where(p_odd == 1, 0, 1)
    cross = jnp.where(lane < LANES // 2, vert_swap, q_odd) == 1
    for k in range(4):
        begin = pl.multiple_of(starts[k], side)
        for c in range(2):
            left = map_ref[c, pl.ds(begin, side), :LANES]
            right = map_ref[c, pl.ds(begin, side), LANES:]
            own0[c, k * side : (k + 1) * side, :LANES] = jnp.where(cross, right, left)
            own0[c, k * side : (k + 1) * side, LANES : 2 * LANES] = jnp.where(cross, left, right)
            own0[c, k * side : (k + 1) * side, 2 * LANES :] = out_ref[c, pl.ds(begin, side), :]

    first = remote(own0.at[:, :side], face1, send1, recv1, (vertical, q))
    first.start()
    first.wait()

    mine = own0[0, :side], own0[1, :side]
    theirs = face1[0], face1[1]
    across = embed_low(tile(theirs[0], 0), tile(theirs[1], 0))
    stacked = rows(theirs)
    product = dot3(across, rows(mine))
    turned = tile(product, 0)
    inv = inverse(embed_low(turned[:side], turned[side:]), pow_ref, inv_ref)
    right_part = cols([
        jnp.where(low_lanes(turned.shape), half_roll(turned), -tile(stacked, 0)),
        tile(product, 1),
        -tile(stacked, 1),
        tile(product, 2) - tile(stacked, 2),
    ])
    wave = dot3(inv, right_part)
    rest = own0[0, side:], own0[1, side:]
    gain = dot3(embed_low(tile(rest[0], 0), tile(rest[1], 0)), wave)
    count = 3 * side
    for c in range(2):
        part = gain[c * count : (c + 1) * count]
        first_tile = tile(rest[c], 0)
        x1[c, :, :LANES] = tile(part, 0) + jnp.where(
            low_lanes(first_tile.shape), half_roll(first_tile), 0.0
        )
        x1[c, :, LANES : 2 * LANES] = tile(part, 1) + tile(rest[c], 1)
        x1[c, :, 2 * LANES : 3 * LANES] = tile(part, 2)
        x1[c, :, 3 * LANES :] = tile(part, 3) + tile(rest[c], 2)

    to_vert = remote(x1.at[:, :side], face2.at[0], send2.at[0], recv2.at[0], (vertical, q))
    to_side = remote(x1.at[:, :side], face2.at[1], send2.at[1], recv2.at[1], (p, beside))
    to_vert.start()
    to_side.start()
    to_vert.wait_recv()
    relay = remote(face2.at[0], face2.at[2], send2.at[2], recv2.at[2], (p, beside))
    relay.start()
    to_side.wait_recv()
    relay.wait_recv()
    to_vert.wait_send()
    to_side.wait_send()
    relay.wait_send()
    mine = [rows([x1[c, :side], swapped_view(face2[0, c])]) for c in range(2)]
    theirs = [rows([face2[1, c], swapped_view(face2[2, c])]) for c in range(2)]
    stacked = rows(theirs)
    product = dot3(embed(tile(theirs[0], 0), tile(theirs[1], 0)), rows(mine))
    turned = tile(product, 0)
    inv = inverse(embed(turned[: 2 * side], turned[2 * side :]), pow_ref, inv_ref)
    right_part = cols([
        tile(product, 1),
        tile(product, 2),
        -tile(stacked, 1),
        -tile(stacked, 2),
        tile(product, 3) - tile(stacked, 3),
    ])
    wave = dot3(inv, right_part)
    rest = x1[0, side:], x1[1, side:]
    gain = dot3(embed(tile(rest[0], 0), tile(rest[1], 0)), wave)
    count = 2 * side
    for c in range(2):
        part = gain[c * count : (c + 1) * count]
        t_own = tile(part, 0) + tile(rest[c], 1)
        t_vert = tile(part, 1) + tile(rest[c], 2)
        t_side = tile(part, 2)
        t_diag = tile(part, 3)
        own_0 = jnp.where(q_odd == 1, t_side, t_own)
        own_1 = jnp.where(q_odd == 1, t_own, t_side)
        vert_0 = jnp.where(q_odd == 1, t_diag, t_vert)
        vert_1 = jnp.where(q_odd == 1, t_vert, t_diag)
        in_0 = jnp.where(inner, own_0, vert_0)
        in_1 = jnp.where(inner, own_1, vert_1)
        out_0 = jnp.where(inner, vert_0, own_0)
        out_1 = jnp.where(inner, vert_1, own_1)
        x2[c, :, :LANES] = low_low(in_0, in_1)
        x2[c, :, LANES : 2 * LANES] = low_low(out_0, out_1)
        x2[c, :, 2 * LANES : 3 * LANES] = jnp.where(
            lower, high_high(out_1, in_1), high_high(in_1, out_1)
        )
        x2[c, :, 3 * LANES : 4 * LANES] = jnp.where(
            lower, high_high(out_0, in_0), high_high(in_0, out_0)
        )
        x2[c, :, 4 * LANES :] = tile(part, 4) + tile(rest[c], 3)

    def send_face(src, box, slot, target):
        return remote(src, face3.at[box, q_odd], send3.at[slot], recv3.at[slot], target)

    up_own = lambda: send_face(x2.at[:, :side], 0, 0, (vertical, q))
    up_other = lambda: send_face(face3.at[1, q_odd], 1, 1, (vertical, q))
    over = lambda: send_face(x2.at[:, :side], 1, 2, (facing, q))

    @pl.when(inner)
    def _():
        over().start()
        up_own().start()
        send_face(x2.at[:, :side], 0, 3, (p, beside)).start()
        face3[0, q_odd] = x2[:, :side]
        over().wait_recv()
        up_other().start()
        side_other = send_face(face3.at[1, q_odd], 1, 4, (p, beside))
        side_other.start()
        over().wait_send()
        up_own().wait_send()
        up_other().wait_send()
        send_face(x2.at[:, :side], 0, 3, (p, beside)).wait()
        side_other.wait()

    @pl.when(jnp.logical_not(inner))
    def _():
        up_own().wait_recv()
        side_own = send_face(face3.at[0, q_odd], 0, 3, (p, beside))
        side_own.start()
        up_other().wait_recv()
        side_other = send_face(face3.at[1, q_odd], 1, 4, (p, beside))
        side_other.start()
        side_own.wait()
        side_other.wait()

    mine = [rows([face3[0, 0, c], face3[0, 1, c]]) for c in range(2)]
    theirs = [rows([face3[1, 0, c], face3[1, 1, c]]) for c in range(2)]
    stacked = rows(theirs)
    product = dot3(embed(tile(theirs[0], 0), tile(theirs[1], 0)), rows(mine))
    turned = tile(product, 0)
    inv = inverse(embed(turned[: 2 * side], turned[2 * side :]), pow_ref, inv_ref)
    right_part = cols([
        tile(product, 1),
        tile(product, 2),
        tile(product, 3),
        -tile(stacked, 1),
        -tile(stacked, 2),
        -tile(stacked, 3),
        tile(product, 4) - tile(stacked, 4),
    ])
    wave = dot3(inv, right_part)
    begin = pl.multiple_of(inner_num * side, side)
    rest = x2[0, pl.ds(begin, side)], x2[1, pl.ds(begin, side)]
    gain = dot3(embed(tile(rest[0], 0), tile(rest[1], 0)), wave)
    for c in range(2):
        part = gain[c * side : (c + 1) * side]
        own = [tile(part, k) + tile(rest[c], k + 1) for k in range(3)]
        other = [tile(part, k + 3) for k in range(3)]
        low = [jnp.where(lower, a, b) for a, b in zip(own, other)]
        up = [jnp.where(lower, b, a) for a, b in zip(own, other)]
        for k, value in enumerate([low[0], low[1], low[2], up[1], up[0], up[2]]):
            top_ref[c, :, k * LANES : (k + 1) * LANES] = value
        top_out_ref[c] = tile(part, 6) + tile(rest[c], 4)


def merge_tree(leaf_map, outgoing):
    order = leaf_map.shape[1]
    side = order // 4
    rhs = outgoing.shape[2]
    vmem = pl.BlockSpec(memory_space=pltpu.VMEM)
    dma = pltpu.SemaphoreType.DMA
    return pl.pallas_call(
        merge_kernel,
        name="merge_tree",
        out_shape=(
            jax.ShapeDtypeStruct((2, side, 12 * side), F32),
            jax.ShapeDtypeStruct((2, side, rhs), F32),
        ),
        in_specs=[vmem, vmem],
        out_specs=(vmem, vmem),
        scratch_shapes=[
            pltpu.VMEM((2, order, order + rhs), F32),
            pltpu.VMEM((2, side, order + rhs), F32),
            pltpu.VMEM((3, 2, side, 6 * side + rhs), F32),
            pltpu.VMEM((2, 3 * side, 6 * side + rhs), F32),
            pltpu.VMEM((2, 2 * side, 8 * side + rhs), F32),
            pltpu.VMEM((2, 2, 2, side, 8 * side + rhs), F32),
            pltpu.VMEM((order, order), F32),
            pltpu.VMEM((order, order), F32),
            dma, dma, dma((3,)), dma((3,)), dma((5,)), dma((5,)),
        ],
        compiler_params=pltpu.CompilerParams(
            collective_id=0, has_side_effects=True, vmem_limit_bytes=48 * 1024 * 1024
        ),
    )(leaf_map, outgoing)


def padded_2(cells, sides, width):
    for axis, dim in sides:
        count = lax.axis_size(axis)
        ends = count - 1
        head = lax.slice_in_dim(cells, 0, width, axis=dim)
        tail = lax.slice_in_dim(cells, cells.shape[dim] - width, cells.shape[dim], axis=dim)
        cells = jnp.concatenate(
            [
                lax.ppermute(tail, axis, [(i, (i + 1) % count) for i in range(ends)]),
                cells,
                lax.ppermute(head, axis, [((i + 1) % count, i) for i in range(ends)]),
            ],
            axis=dim,
        )
    return cells


def residual_of(source, padded, coefficient):
    center = padded[1:-1, 1:-1]
    beside_all = padded[2:, 1:-1] + padded[:-2, 1:-1] + padded[1:-1, 2:] + padded[1:-1, :-2]
    wave_term = coefficient[:, :, None]
    diagonal_term = 4.0 - wave_term
    real_part = (
        diagonal_term * center[:, :, 0]
        + wave_term * DAMPING * center[:, :, 1]
        - beside_all[:, :, 0]
    )
    imag_part = (
        diagonal_term * center[:, :, 1]
        - wave_term * DAMPING * center[:, :, 0]
        - beside_all[:, :, 1]
    )
    applied = jnp.stack([real_part, imag_part], axis=2)
    return (source.astype(jnp.float32) - applied).astype(jnp.bfloat16)


def on_device(source, guess, coefficient, leaf_map, body_map):
    padded = padded_2(guess, (("tx", 0), ("ty", 1)), 1).astype(jnp.float32)
    residual = residual_of(source, padded, coefficient)
    tile_len = guess.shape[0]
    cells = residual.reshape(tile_len * tile_len, 2, guess.shape[3])
    products = jnp.einsum(
        "ack,kbr->abcr", body_map[0, 0], cells, preferred_element_type=jnp.float32
    )
    outgoing = jnp.stack([products[0, 0] - products[1, 1], products[0, 1] + products[1, 0]])
    own_map, own_out = merge_tree(leaf_map[0, 0], outgoing)
    return (own_map[None, None], own_out[None, None])


def solution(mesh):
    placed = (
        P("tx", "ty", None, None),
        P("tx", "ty", None, None),
        P("tx", "ty"),
        P("tx", "ty", None, None, None),
        P("tx", "ty", None, None, None),
    )
    return jax.shard_map(
        on_device,
        mesh=mesh,
        in_specs=placed,
        out_specs=(P("tx", "ty", None, None, None), P("tx", "ty", None, None, None)),
        check_vma=False,
    )
```

profile of v0, /device:TPU:0, one launch (start us, length us, event | category | flops | bytes accessed | tf_op | source)
XLA Modules:
  0.0 102.4 jit_solution(1994499879674209959)
XLA Ops:
  0.6 0.8 fusion.12
  1.5 5.0 %collective-permute-start = (bf16[1,64,2,128]{3,2,1,0:T(2,128)(2,1)S(1)}, bf16[1,64,2,128]{3,2,1,0:T(2,128)(2,1)S(1)}, u32[]{:S(2)}, u32[]{:S(2)}) collective-permute-start(bf16[1,64,2,128]{3,2,1,0:T(2,128)(2,1)S(1)} %get-tuple-element.11), channel_id=1, source_target_pairs={{0,8},{8,16},{16,24},{1,9},{9,17},{17,25},{2,10},{10,18},{18,26},{... | collective-permute-start | bytes 98312 | tf_op jit(solution)/shard_map/ppermute | solution.py:336
  6.4 1.3 %collective-permute-start.1 = (bf16[1,64,2,128]{3,2,1,0:T(2,128)(2,1)S(1)}, bf16[1,64,2,128]{3,2,1,0:T(2,128)(2,1)S(1)}, u32[]{:S(2)}, u32[]{:S(2)}) collective-permute-start(bf16[1,64,2,128]{3,2,1,0:T(2,128)(2,1)S(1)} %get-tuple-element.10), channel_id=1, source_target_pairs={{8,0},{16,8},{24,16},{9,1},{17,9},{25,17},{10,2},{18,10},{26,18},{... | collective-permute-start | bytes 98312 | tf_op jit(solution)/shard_map/ppermute | solution.py:338
  7.7 0.3 collective-permute-done
  8.0 0.0 copy-start.2
  8.0 4.8 %constant_dynamic-update-slice_fusion.1 = bf16[66,64,2,128]{3,2,1,0:T(2,128)(2,1)S(1)} fusion(bf16[66,64,2,128]{3,2,1,0:T(2,128)(2,1)S(1)} %constant_dynamic-update-slice_fusion.2, bf16[64,64,2,128]{3,2,1,0:T(2,128)(2,1)} %param.6), kind=kLoop, calls=%fused_computation.20 | loop fusion | bytes 4194304
  12.9 0.0 collective-permute-done.1
  12.9 0.1 fusion.11
  13.0 1.3 %collective-permute-start.2 = (bf16[66,1,2,128]{3,2,1,0:T(2,128)(2,1)S(1)}, bf16[66,1,2,128]{3,2,1,0:T(2,128)(2,1)S(1)}, u32[]{:S(2)}, u32[]{:S(2)}) collective-permute-start(bf16[66,1,2,128]{3,2,1,0:T(2,128)(2,1)S(1)} %get-tuple-element.8), channel_id=1, source_target_pairs={{0,1},{1,2},{2,3},{3,4},{4,5},{5,6},{6,7},{8,9},{9,10},{10,11},{11... | collective-permute-start | bytes 101384 | tf_op jit(solution)/shard_map/ppermute | solution.py:336
  14.3 1.3 %collective-permute-start.3 = (bf16[66,1,2,128]{3,2,1,0:T(2,128)(2,1)S(1)}, bf16[66,1,2,128]{3,2,1,0:T(2,128)(2,1)S(1)}, u32[]{:S(2)}, u32[]{:S(2)}) collective-permute-start(bf16[66,1,2,128]{3,2,1,0:T(2,128)(2,1)S(1)} %get-tuple-element.9), channel_id=1, source_target_pairs={{1,0},{2,1},{3,2},{4,3},{5,4},{6,5},{7,6},{9,8},{10,9},{11,10},{12... | collective-permute-start | bytes 101384 | tf_op jit(solution)/shard_map/ppermute | solution.py:338
  15.6 0.0 copy-done.2
  15.6 0.0 collective-permute-done.2
  15.6 3.5 %collective-permute-done.3 = bf16[66,1,2,128]{3,2,1,0:T(2,128)(2,1)S(1)} collective-permute-done((bf16[66,1,2,128]{3,2,1,0:T(2,128)(2,1)S(1)}, bf16[66,1,2,128]{3,2,1,0:T(2,128)(2,1)S(1)}, u32[]{:S(2)}, u32[]{:S(2)}) %collective-permute-start.3) | collective-permute-done | bytes 33824 | tf_op jit(solution)/shard_map/ppermute | solution.py:338
  19.1 3.2 %maximum_convert_fusion = f32[66,66,2,128]{3,2,1,0:T(2,128)S(1)} fusion(bf16[66,1,2,128]{3,2,1,0:T(2,128)(2,1)S(1)} %collective-permute-done.3, bf16[66,64,2,128]{3,2,1,0:T(2,128)(2,1)S(1)} %constant_dynamic-update-slice_fusion, bf16[66,1,2,128]{3,2,1,0:T(2,128)(2,1)S(1)} %collective-permute-done.2), kind=kLoop, calls=%fused_computation.7 | loop fusion | flops 3345408 | bytes 6690816 | tf_op jit(solution)/shard_map/convert_element_type | solution.py:365
  22.3 3.7 %slice_add_fusion = f32[64,64,2,128]{3,2,1,0:T(2,128)S(1)} fusion(f32[66,66,2,128]{3,2,1,0:T(2,128)S(1)} %maximum_convert_fusion), kind=kLoop, calls=%fused_computation | loop fusion | flops 3145728 | bytes 20971520 | tf_op jit(solution)/shard_map/add | solution.py:347
  26.0 0.0 copy-start.1
  26.0 11.3 %slice_subtract_fusion.1 = (f32[64,64,1,128]{3,2,1,0:T(1,128)S(1)}, f32[64,64,1,128]{3,2,1,0:T(1,128)S(1)}) fusion(f32[64,64,2,128]{3,2,1,0:T(2,128)S(1)} %slice_add_fusion, f32[66,66,2,128]{3,2,1,0:T(2,128)S(1)} %maximum_convert_fusion, f32[64,64]{1,0:T(8,128)S(1)} %get-tuple-element.15, f32[64,64]{1,0:T(8,128)S(1)} %get-tuple-element.14), kind=kLoop, calls=%fused_computation.9 | loop fusion | flops 4194304 | bytes 12615680 | tf_op jit(solution)/shard_map/sub | solution.py:351
  37.3 0.0 copy-done.1
  37.3 5.2 %fusion = bf16[64,64,2,128]{3,2,1,0:T(2,128)(2,1)S(1)} fusion(f32[64,64,1,128]{3,2,1,0:T(1,128)S(1)} %get-tuple-element.7, f32[64,64,1,128]{3,2,1,0:T(1,128)S(1)} %get-tuple-element.6, bf16[64,64,2,128]{3,2,1,0:T(2,128)(2,1)S(1)} %copy-done.1), kind=kLoop, calls=%fused_computation.4 | loop fusion | flops 4194304 | bytes 8388608 | tf_op jit(solution)/shard_map/convert_element_type | solution.py:361
  42.5 4.0 %copy.7 = bf16[4096,2,128]{0,2,1:T(8,128)(2,1)} copy(bf16[4096,2,128]{2,1,0:T(2,128)(2,1)S(1)} %bitcast.27) | data formatting | bytes 4194304 | tf_op jit(solution)/shard_map/reshape | solution.py:368
  46.4 0.0 copy-start
  46.4 4.2 %fusion.4 = f32[2,2,256,128]{3,2,1,0:T(8,128)S(1)} fusion(bf16[1,1,2,256,4096]{4,3,2,1,0:T(8,128)(2,1)} %param.9, bf16[4096,2,128]{0,2,1:T(8,128)(2,1)} %copy.7), kind=kOutput, calls=%fused_computation.11 | convolution fusion | flops 1073741824 | bytes 6815744 | tf_op jit(solution)/shard_map/ack,kbr->abcr/dot_general | solution.py:369
  50.7 0.0 copy-done
  50.7 50.4 %merge_tree.1 = (f32[2,64,768]{2,1,0:T(8,128)S(1)}, f32[2,64,128]{2,1,0:T(8,128)S(1)}) custom-call(f32[2,256,256]{2,1,0:T(8,128)S(1)} %bitcast.24, f32[2,256,128]{2,1,0:T(8,128)S(1)} %pad_maximum_fusion.out_ref), custom_call_target="tpu_custom_call" | custom-call | tf_op jit(solution)/shard_map/merge_tree/pallas_call | solution.py:302
  101.0 0.7 copy.15
  101.8 0.6 copy.16
  (5 shorter events, 0.1 us)
Async XLA Ops:
  1.5 6.5 %collective-permute-start = (bf16[1,64,2,128]{3,2,1,0:T(2,128)(2,1)S(1)}, bf16[1,64,2,128]{3,2,1,0:T(2,128)(2,1)S(1)}, u32[]{:S(2)}, u32[]{:S(2)}) collective-permute-start(bf16[1,64,2,128]{3,2,1,0:T(2,128)(2,1)S(1)} %get-tuple-element.11), channel_id=1, source_target_pairs={{0,8},{8,16},{16,24},{1,9},{9,17},{17,25},{2,10},{10,18},{18,26},{... | collective-permute-start | bytes 98312 | tf_op jit(solution)/shard_map/ppermute | solution.py:336
  6.4 6.5 %collective-permute-start.1 = (bf16[1,64,2,128]{3,2,1,0:T(2,128)(2,1)S(1)}, bf16[1,64,2,128]{3,2,1,0:T(2,128)(2,1)S(1)}, u32[]{:S(2)}, u32[]{:S(2)}) collective-permute-start(bf16[1,64,2,128]{3,2,1,0:T(2,128)(2,1)S(1)} %get-tuple-element.10), channel_id=1, source_target_pairs={{8,0},{16,8},{24,16},{9,1},{17,9},{25,17},{10,2},{18,10},{26,18},{... | collective-permute-start | bytes 98312 | tf_op jit(solution)/shard_map/ppermute | solution.py:338
  8.0 7.6 %copy-start.2 = (f32[64,64]{1,0:T(8,128)S(1)}, f32[64,64]{1,0:T(8,128)}, u32[]{:S(2)}) copy-start(f32[64,64]{1,0:T(8,128)} %param.7) | copy-start | bytes 49156
  13.0 2.6 %collective-permute-start.2 = (bf16[66,1,2,128]{3,2,1,0:T(2,128)(2,1)S(1)}, bf16[66,1,2,128]{3,2,1,0:T(2,128)(2,1)S(1)}, u32[]{:S(2)}, u32[]{:S(2)}) collective-permute-start(bf16[66,1,2,128]{3,2,1,0:T(2,128)(2,1)S(1)} %get-tuple-element.8), channel_id=1, source_target_pairs={{0,1},{1,2},{2,3},{3,4},{4,5},{5,6},{6,7},{8,9},{9,10},{10,11},{11... | collective-permute-start | bytes 101384 | tf_op jit(solution)/shard_map/ppermute | solution.py:336
  14.3 4.8 %collective-permute-start.3 = (bf16[66,1,2,128]{3,2,1,0:T(2,128)(2,1)S(1)}, bf16[66,1,2,128]{3,2,1,0:T(2,128)(2,1)S(1)}, u32[]{:S(2)}, u32[]{:S(2)}) collective-permute-start(bf16[66,1,2,128]{3,2,1,0:T(2,128)(2,1)S(1)} %get-tuple-element.9), channel_id=1, source_target_pairs={{1,0},{2,1},{3,2},{4,3},{5,4},{6,5},{7,6},{9,8},{10,9},{11,10},{12... | collective-permute-start | bytes 101384 | tf_op jit(solution)/shard_map/ppermute | solution.py:338
  26.0 11.3 %copy-start.1 = (bf16[64,64,2,128]{3,2,1,0:T(2,128)(2,1)S(1)}, bf16[64,64,2,128]{3,2,1,0:T(2,128)(2,1)}, u32[]{:S(2)}) copy-start(bf16[64,64,2,128]{3,2,1,0:T(2,128)(2,1)} %param.5) | copy-start | bytes 6291460
  46.4 4.2 %copy-start = (f32[1,1,2,256,256]{4,3,2,1,0:T(8,128)S(1)}, f32[1,1,2,256,256]{4,3,2,1,0:T(8,128)}, u32[]{:S(2)}) copy-start(f32[1,1,2,256,256]{4,3,2,1,0:T(8,128)} %param.8) | copy-start | bytes 1572868
where the time goes:
time: 103 us; the launch traced here: 102 us
  Pallas kernels  50.4 us (49%)
  other arithmetic  23.4 us (23%)
  local copies, waits for them, and re-layouts  11.1 us (11%)
  starting transfers between devices  8.83 us (9%)
  matrix products  4.16 us (4%)
  waiting for transfers between devices  3.77 us (4%)
    pallas_call x1, Pallas kernels, merge_tree(): pl.pallas_call(merge_kernel, name='merge_tree', out_shape=(jax.ShapeDtype...  50.4 us
    sub x1, other arithmetic, residual_of(): diagonal_term * center[:, :, 0] + wave_term * DAMPING * center[:, :, 1]  11.3 us
    ppermute x2, starting transfers between devices, padded_2(): lax.ppermute(tail, axis, [(i, (i + 1) % count) for i in range(ends)])  6.25 us
    unnamed x10, local copies, waits for them, and re-layouts  6.24 us
    convert_element_type x1, other arithmetic, residual_of(): return (source.astype(jnp.float32) - applied).astype(jnp.bfloat16)  5.19 us
    dot_general x1, matrix products, on_device(): jnp.einsum('ack,kbr->abcr', body_map[0, 0], cells, preferred_element_type...  4.16 us
    reshape x1, local copies, waits for them, and re-layouts, on_device(): cells = residual.reshape(tile_len * tile_len, 2, guess.shape[3])  3.96 us
    add x1, other arithmetic, residual_of(): padded[2:, 1:-1] + padded[:-2, 1:-1] + padded[1:-1, 2:] + padded[1:-1, :-2]  3.69 us
  transfers between devices with their start and end apart: 4, of which 2 were waited for; matrix products, arithmetic and copies ran while one was open for 5% of the time, Pallas kernels for 0%

commit v1 on v0

v1 whole, which is shorter than its diff:
```python
import functools

import jax
import jax.numpy as jnp
from jax import lax
from jax.experimental import pallas as pl
from jax.experimental.pallas import tpu as pltpu
from jax.sharding import PartitionSpec as P

DAMPING = 0.5
DOUBLINGS = 7
LANES = 128
MESH = pl.DeviceIdType.MESH
F32 = jnp.float32
BF16 = jnp.bfloat16
WIRE = F32


def split(x):
    high = x.astype(BF16)
    return high, (x - high.astype(F32)).astype(BF16)


def dot1(a, b):
    return jnp.dot(a, b, preferred_element_type=F32)


def dot3(a, b):
    a_high, a_low = split(a)
    b_high, b_low = split(b)
    return dot1(a_high, b_high) + (dot1(a_high, b_low) + dot1(a_low, b_high))


def tile(x, k):
    return x[:, k * LANES : (k + 1) * LANES]


def cols(parts):
    return jnp.concatenate(parts, axis=1)


def rows(parts):
    return jnp.concatenate(parts, axis=0)


def half_roll(x):
    return pltpu.roll(x, LANES // 2, 1)


def low_lanes(shape):
    return lax.broadcasted_iota(jnp.int32, shape, 1) < LANES // 2


def low_low(a, b):
    return jnp.where(low_lanes(a.shape), a, half_roll(b))


def high_high(a, b):
    return jnp.where(low_lanes(a.shape), half_roll(a), b)


def embed(re, im):
    return rows([cols([re, -im]), cols([im, re])])


def embed_low(re, im):
    return rows([low_low(re, -im), low_low(im, re)])


def identity(n):
    return (
        lax.broadcasted_iota(jnp.int32, (n, n), 0) == lax.broadcasted_iota(jnp.int32, (n, n), 1)
    ).astype(F32)


def inverse(power, pow_ref, inv_ref):
    n = power.shape[0]
    pow_ref[:n, :n] = dot3(power, power)
    inv_ref[:n, :n] = identity(n) + power

    def body(k, carry):
        now, total = pow_ref[:n, :n], inv_ref[:n, :n]
        both = dot3(now, cols([now, total]))
        pow_ref[:n, :n] = both[:, :n]
        inv_ref[:n, :n] = total + both[:, n:]
        return carry

    lax.fori_loop(0, DOUBLINGS - 2, body, 0)
    total = inv_ref[:n, :n]
    return total + dot3(pow_ref[:n, :n], total)


def swapped_view(block):
    return cols([half_roll(tile(block, 0)), tile(block, 2), tile(block, 1)])


def tree_kernel(
    guess_ref, guess_rows_ref, source_ref, coef_ref, map_ref, body_ref, top_ref, top_out_ref,
    guess_v, source_v, body_v, edge_v, beside_v, coef_v, plain, field, load_a, load_b,
    m0, h0, m1, h1, m2, h2, out2, out3,
    face1, face1h, face2, face2h, face3, face3h, pow_ref, inv_ref, cross1, cross2, cross3,
    local_sem, halo_send, halo_recv, send1, recv1, send2, recv2, send3, recv3,
):
    p = lax.axis_index("tx")
    q = lax.axis_index("ty")
    p_ends = lax.axis_size("tx") - 1
    q_ends = lax.axis_size("ty") - 1
    p_low = lax.rem(p, 4)
    p_odd = lax.rem(p, 2)
    q_odd = lax.rem(q, 2)
    vertical = p + 1 - 2 * p_odd
    beside = q + 1 - 2 * q_odd
    inner = (p_low == 1) | (p_low == 2)
    inner_num = jnp.where(inner, 1, 0)
    lower = p_low < 2
    facing = p + 3 - 2 * p_low
    side = map_ref.shape[1] // 4
    length = guess_ref.shape[0]
    last = length - 1

    def remote(src, dst, send, recv, target):
        return pltpu.make_async_remote_copy(
            src_ref=src, dst_ref=dst, send_sem=send, recv_sem=recv,
            device_id=target, device_id_type=MESH,
        )

    halos = [
        (p < p_ends, p > 0, (p + 1, q),
         lambda: remote(guess_rows_ref.at[last], edge_v.at[0], halo_send.at[0], halo_recv.at[0], (p + 1, q))),
        (p > 0, p < p_ends, (p - 1, q),
         lambda: remote(guess_rows_ref.at[0], edge_v.at[1], halo_send.at[1], halo_recv.at[1], (p - 1, q))),
        (q < q_ends, q > 0, (p, q + 1),
         lambda: remote(guess_ref.at[:, last], beside_v.at[0], halo_send.at[2], halo_recv.at[2], (p, q + 1))),
        (q > 0, q < q_ends, (p, q - 1),
         lambda: remote(guess_ref.at[:, 0], beside_v.at[1], halo_send.at[3], halo_recv.at[3], (p, q - 1))),
    ]
    locals_ = [
        pltpu.make_async_copy(guess_rows_ref, guess_v, local_sem.at[0]),
        pltpu.make_async_copy(source_ref, source_v, local_sem.at[1]),
        pltpu.make_async_copy(body_ref, body_v, local_sem.at[2]),
    ]
    for copy in locals_:
        copy.start()
    barrier = pltpu.get_barrier_semaphore()
    arrivals = 0
    for exists, _, target, _ in halos:
        arrivals = arrivals + jnp.where(exists, 1, 0)

        @pl.when(exists)
        def _():
            pl.semaphore_signal(barrier, inc=1, device_id=target, device_id_type=MESH)

    pl.semaphore_wait(barrier, arrivals)
    for exists, _, _, copy in halos:

        @pl.when(exists)
        def _():
            copy().start()

    starts = [
        jnp.where(p_odd == 1, 0, 2 * side),
        jnp.where(q_odd == 1, 3 * side, side),
        jnp.where(p_odd == 1, 2 * side, 0),
        jnp.where(q_odd == 1, side, 3 * side),
    ]
    starts = [pl.multiple_of(begin, side) for begin in starts]
    lane = lax.broadcasted_iota(jnp.int32, (side, LANES), 1)
    vert_swap = jnp.where(p_odd == 1, 0, 1)
    cross = jnp.where(lane < LANES // 2, vert_swap, q_odd) == 1

    first = remote(m0.at[:, :side], face1, send1.at[0], recv1.at[0], (vertical, q))
    for k in range(4):
        for c in range(2):
            left = map_ref[c, pl.ds(starts[k], side), :LANES]
            right = map_ref[c, pl.ds(starts[k], side), LANES:]
            m0[c, k * side : (k + 1) * side, :LANES] = jnp.where(cross, right, left)
            m0[c, k * side : (k + 1) * side, LANES:] = jnp.where(cross, left, right)
        if k == 0:
            first.start()

    pad = 8
    locals_[0].wait()

    def apart(k, carry):
        plain[...] = guess_v[k].astype(F32)
        for c in range(2):
            field[c, k + 1, pad : pad + length] = plain[pl.ds(c, length, 2), :]
        return carry

    lax.fori_loop(0, length, apart, 0)
    coef_v[...] = jnp.zeros_like(coef_v)
    coef_v[:length, :length] = coef_ref[...]
    coef_t = jnp.transpose(coef_v[...])[:length]
    coef_v[:length] = coef_t
    for num, (exists, arrives, _, copy) in enumerate(halos):

        @pl.when(arrives)
        def _():
            copy().wait_recv()
            if num < 2:
                plain[...] = edge_v[num].astype(F32)
                for c in range(2):
                    field[c, (0, length + 1)[num], pad : pad + length] = plain[pl.ds(c, length, 2), :]
            else:
                strip = beside_v[num - 2].astype(F32)
                at = (pad - 1, pad + length)[num - 2]
                for c in range(2):
                    field[c, 1 : length + 1, at : at + 1] = strip[:, c : c + 1]

        @pl.when(jnp.logical_not(arrives))
        def _():
            for c in range(2):
                if num < 2:
                    field[c, (0, length + 1)[num], pad : pad + length] = jnp.zeros((length, LANES), F32)
                else:
                    at = (pad - 1, pad + length)[num - 2]
                    field[c, 1 : length + 1, at : at + 1] = jnp.zeros((length, 1, LANES), F32)

    locals_[1].wait()

    def residual_row(k, carry):
        plain[...] = source_v[k].astype(F32)
        wave_term = jnp.broadcast_to(
            pltpu.roll(coef_v[:length], lax.rem(LANES - k, LANES), 1)[:, :1], (length, LANES)
        )
        diagonal_term = 4.0 - wave_term
        damp = wave_term * DAMPING
        center = [field[c, k + 1, pad : pad + length] for c in range(2)]
        around = [
            field[c, k + 2, pad : pad + length]
            + field[c, k, pad : pad + length]
            + field[c, k + 1, pad + 1 : pad + 1 + length]
            + field[c, k + 1, pad - 1 : pad - 1 + length]
            for c in range(2)
        ]
        real_part = diagonal_term * center[0] + damp * center[1] - around[0]
        imag_part = diagonal_term * center[1] - damp * center[0] - around[1]
        real = (plain[pl.ds(0, length, 2), :] - real_part).astype(BF16)
        imag = (plain[pl.ds(1, length, 2), :] - imag_part).astype(BF16)
        at = pl.ds(pl.multiple_of(k * length, length), length)
        load_a[at, :LANES] = real
        load_a[at, LANES:] = imag
        load_b[at, :LANES] = -imag
        load_b[at, LANES:] = real
        return carry

    lax.fori_loop(0, length, residual_row, 0)

    first.wait()
    mine = rows([m0[0, :side], m0[1, :side]])
    theirs = rows([face1[0], face1[1]])
    across = embed_low(theirs[:side, :LANES], theirs[side:, :LANES])
    cross1[0] = across
    product = dot3(across, mine)
    turned = tile(product, 0)
    inv = inverse(embed_low(turned[:side], turned[side:]), pow_ref, inv_ref)
    cross1[1] = inv
    wave = dot3(inv, cols([
        jnp.where(low_lanes(turned.shape), half_roll(turned), -tile(theirs, 0)),
        tile(product, 1),
        -tile(theirs, 1),
    ]))
    rest = m0[0, side:], m0[1, side:]
    gain = dot3(embed_low(tile(rest[0], 0), tile(rest[1], 0)), wave)
    count = 3 * side
    for c in range(2):
        part = gain[c * count : (c + 1) * count]
        first_tile = tile(rest[c], 0)
        m1[c, :, :LANES] = tile(part, 0) + jnp.where(
            low_lanes(first_tile.shape), half_roll(first_tile), 0.0
        )
        m1[c, :, LANES : 2 * LANES] = tile(part, 1) + tile(rest[c], 1)
        m1[c, :, 2 * LANES :] = tile(part, 2)
    out2[...] = m1[:, :side].astype(WIRE)

    def exchange(src, face, kind):
        return (
            remote(src, face.at[0], send2.at[kind, 0], recv2.at[kind, 0], (vertical, q)),
            remote(src, face.at[1], send2.at[kind, 1], recv2.at[kind, 1], (p, beside)),
            remote(face.at[0], face.at[2], send2.at[kind, 2], recv2.at[kind, 2], (p, beside)),
        )

    maps2 = exchange(out2, face2, 0)
    maps2[0].start()
    maps2[1].start()

    locals_[2].wait()
    leaf = dot1(body_v[0], load_a[...]) + dot1(body_v[1], load_b[...])
    inv_ref[...] = leaf
    for k in range(4):
        for c in range(2):
            h0[c, k * side : (k + 1) * side] = inv_ref[
                pl.ds(starts[k], side), c * LANES : (c + 1) * LANES
            ]
    first_h = remote(h0.at[:, :side], face1h, send1.at[1], recv1.at[1], (vertical, q))
    first_h.start()
    maps2[0].wait_recv()
    maps2[2].start()
    first_h.wait()
    wave = dot3(
        cross1[1],
        dot3(cross1[0], rows([h0[0, :side], h0[1, :side]])) - rows([face1h[0], face1h[1]]),
    )
    rest = m0[0, side:], m0[1, side:]
    gain = dot3(embed_low(tile(rest[0], 0), tile(rest[1], 0)), wave)
    for c in range(2):
        h1[c] = gain[c * count : (c + 1) * count] + h0[c, side:]
    data2 = exchange(h1.at[:, :side], face2h, 1)
    data2[0].start()
    data2[1].start()

    maps2[1].wait_recv()
    maps2[2].wait_recv()
    for copy in maps2:
        copy.wait_send()
    mine = rows([
        x for c in range(2) for x in (m1[c, :side], swapped_view(face2[0, c].astype(F32)))
    ])
    theirs = rows([
        x
        for c in range(2)
        for x in (face2[1, c].astype(F32), swapped_view(face2[2, c].astype(F32)))
    ])
    across = embed(theirs[: 2 * side, :LANES], theirs[2 * side :, :LANES])
    cross2[0] = across
    product = dot3(across, mine)
    turned = tile(product, 0)
    inv = inverse(embed(turned[: 2 * side], turned[2 * side :]), pow_ref, inv_ref)
    cross2[1] = inv
    wave = dot3(inv, cols([
        tile(product, 1), tile(product, 2), -tile(theirs, 1), -tile(theirs, 2),
    ]))
    rest = m1[0, side:], m1[1, side:]
    gain = dot3(embed(tile(rest[0], 0), tile(rest[1], 0)), wave)
    count2 = 2 * side
    for c in range(2):
        part = gain[c * count2 : (c + 1) * count2]
        t_own = tile(part, 0) + tile(rest[c], 1)
        t_vert = tile(part, 1) + tile(rest[c], 2)
        t_side = tile(part, 2)
        t_diag = tile(part, 3)
        own_0 = jnp.where(q_odd == 1, t_side, t_own)
        own_1 = jnp.where(q_odd == 1, t_own, t_side)
        vert_0 = jnp.where(q_odd == 1, t_diag, t_vert)
        vert_1 = jnp.where(q_odd == 1, t_vert, t_diag)
        in_0 = jnp.where(inner, own_0, vert_0)
        in_1 = jnp.where(inner, own_1, vert_1)
        out_0 = jnp.where(inner, vert_0, own_0)
        out_1 = jnp.where(inner, vert_1, own_1)
        m2[c, :, :LANES] = low_low(in_0, in_1)
        m2[c, :, LANES : 2 * LANES] = low_low(out_0, out_1)
        m2[c, :, 2 * LANES : 3 * LANES] = jnp.where(
            lower, high_high(out_1, in_1), high_high(in_1, out_1)
        )
        m2[c, :, 3 * LANES :] = jnp.where(
            lower, high_high(out_0, in_0), high_high(in_0, out_0)
        )
    out3[...] = m2[:, :side].astype(WIRE)

    def last_copies(src, face, kind):
        def send(source, box, slot, target):
            return remote(
                source, face.at[box, q_odd], send3.at[kind, slot], recv3.at[kind, slot], target
            )

        return (
            lambda: send(src, 0, 0, (vertical, q)),
            lambda: send(face.at[1, q_odd], 1, 1, (vertical, q)),
            lambda: send(src, 1, 2, (facing, q)),
            lambda: send(src, 0, 3, (p, beside)),
            lambda: send(face.at[0, q_odd], 0, 3, (p, beside)),
            lambda: send(face.at[1, q_odd], 1, 4, (p, beside)),
        )

    def last_start(copies, src, face):
        up_own, up_other, over, side_own, side_relay, side_other = copies

        @pl.when(inner)
        def _():
            over().start()
            up_own().start()
            side_own().start()
            face[0, q_odd] = src[:, :side]

    def last_relay(copies):
        up_own, up_other, over, side_own, side_relay, side_other = copies

        @pl.when(inner)
        def _():
            over().wait_recv()
            up_other().start()
            side_other().start()

        @pl.when(jnp.logical_not(inner))
        def _():
            up_own().wait_recv()
            side_relay().start()
            up_other().wait_recv()
            side_other().start()

    def last_wait(copies):
        up_own, up_other, over, side_own, side_relay, side_other = copies
        side_own().wait_recv()
        side_other().wait_recv()

    def last_drain(copies):
        up_own, up_other, over, side_own, side_relay, side_other = copies
        side_own().wait_send()
        side_other().wait_send()

        @pl.when(inner)
        def _():
            over().wait_send()
            up_own().wait_send()
            up_other().wait_send()

    maps3 = last_copies(out3, face3, 0)
    last_start(maps3, out3, face3)

    data2[0].wait_recv()
    data2[2].start()
    data2[1].wait_recv()
    data2[2].wait_recv()
    mine = rows([x for c in range(2) for x in (h1[c, :side], face2h[0, c])])
    theirs = rows([x for c in range(2) for x in (face2h[1, c], face2h[2, c])])
    wave = dot3(cross2[1], dot3(cross2[0], mine) - theirs)
    rest = m1[0, side:], m1[1, side:]
    gain = dot3(embed(tile(rest[0], 0), tile(rest[1], 0)), wave)
    for c in range(2):
        h2[c] = gain[c * count2 : (c + 1) * count2] + h1[c, side:]
    data3 = last_copies(h2.at[:, :side], face3h, 1)
    last_start(data3, h2, face3h)
    last_relay(maps3)
    last_relay(data3)

    last_wait(maps3)
    mine = rows([face3[0, j, c].astype(F32) for c in range(2) for j in range(2)])
    theirs = rows([face3[1, j, c].astype(F32) for c in range(2) for j in range(2)])
    across = embed(theirs[: 2 * side, :LANES], theirs[2 * side :, :LANES])
    product = dot3(across, mine)
    turned = tile(product, 0)
    inv = inverse(embed(turned[: 2 * side], turned[2 * side :]), pow_ref, inv_ref)
    begin = pl.multiple_of(inner_num * side, side)
    rest = m2[0, pl.ds(begin, side)], m2[1, pl.ds(begin, side)]
    out_gain = dot3(embed(tile(rest[0], 0), tile(rest[1], 0)), inv)
    cross3[0] = across
    cross3[1, : 2 * side] = out_gain
    gain = dot3(out_gain, cols(
        [tile(product, k) for k in range(1, 4)] + [-tile(theirs, k) for k in range(1, 4)]
    ))
    for c in range(2):
        part = gain[c * side : (c + 1) * side]
        own = [tile(part, k) + tile(rest[c], k + 1) for k in range(3)]
        other = [tile(part, k + 3) for k in range(3)]
        low = [jnp.where(lower, a, b) for a, b in zip(own, other)]
        up = [jnp.where(lower, b, a) for a, b in zip(own, other)]
        for k, value in enumerate([low[0], low[1], low[2], up[1], up[0], up[2]]):
            top_ref[c, :, k * LANES : (k + 1) * LANES] = value
    last_wait(data3)
    mine = rows([face3h[0, j, c] for c in range(2) for j in range(2)])
    theirs = rows([face3h[1, j, c] for c in range(2) for j in range(2)])
    gain = dot3(cross3[1, : 2 * side], dot3(cross3[0], mine) - theirs)
    for c in range(2):
        top_out_ref[c] = gain[c * side : (c + 1) * side] + h2[c, pl.ds(begin, side)]
    for copy in data2:
        copy.wait_send()
    last_drain(maps3)
    last_drain(data3)
    for exists, _, _, copy in halos:

        @pl.when(exists)
        def _():
            copy().wait_send()


def on_device(source, guess, coefficient, leaf_map, body_map):
    length, width, _, rhs = guess.shape
    order = leaf_map.shape[3]
    side = order // 4
    vmem = pl.BlockSpec(memory_space=pltpu.VMEM)
    hbm = pl.BlockSpec(memory_space=pl.ANY)
    dma = pltpu.SemaphoreType.DMA
    rows_of = lambda x: x.reshape(length, 2 * width, rhs)
    own_map, own_out = pl.pallas_call(
        tree_kernel,
        name="build_tree",
        out_shape=(
            jax.ShapeDtypeStruct((2, side, 12 * side), F32),
            jax.ShapeDtypeStruct((2, side, rhs), F32),
        ),
        in_specs=[hbm, hbm, hbm, vmem, vmem, hbm],
        out_specs=(vmem, vmem),
        scratch_shapes=[
            pltpu.VMEM((length, 2 * width, rhs), BF16),
            pltpu.VMEM((length, 2 * width, rhs), BF16),
            pltpu.VMEM((2, order, length * width), BF16),
            pltpu.VMEM((2, 2 * width, rhs), BF16),
            pltpu.VMEM((2, length, 2, rhs), BF16),
            pltpu.VMEM((LANES, LANES), F32),
            pltpu.VMEM((2 * width, rhs), F32),
            pltpu.VMEM((2, length + 2, width + 16, rhs), F32),
            pltpu.VMEM((length * width, 2 * rhs), BF16),
            pltpu.VMEM((length * width, 2 * rhs), BF16),
            pltpu.VMEM((2, order, order), F32),
            pltpu.VMEM((2, order, rhs), F32),
            pltpu.VMEM((2, 3 * side, 6 * side), F32),
            pltpu.VMEM((2, 3 * side, rhs), F32),
            pltpu.VMEM((2, 2 * side, 8 * side), F32),
            pltpu.VMEM((2, 2 * side, rhs), F32),
            pltpu.VMEM((2, side, 6 * side), WIRE),
            pltpu.VMEM((2, side, 8 * side), WIRE),
            pltpu.VMEM((2, side, order), F32),
            pltpu.VMEM((2, side, rhs), F32),
            pltpu.VMEM((3, 2, side, 6 * side), WIRE),
            pltpu.VMEM((3, 2, side, rhs), F32),
            pltpu.VMEM((2, 2, 2, side, 8 * side), WIRE),
            pltpu.VMEM((2, 2, 2, side, rhs), F32),
            pltpu.VMEM((order, order), F32),
            pltpu.VMEM((order, order), F32),
            pltpu.VMEM((2, 2 * side, 2 * side), F32),
            pltpu.VMEM((2, order, order), F32),
            pltpu.VMEM((2, order, order), F32),
            dma((3,)), dma((4,)), dma((4,)), dma((2,)), dma((2,)),
            dma((2, 3)), dma((2, 3)), dma((2, 5)), dma((2, 5)),
        ],
        compiler_params=pltpu.CompilerParams(
            collective_id=0, has_side_effects=True, vmem_limit_bytes=56 * 1024 * 1024
        ),
    )(guess, rows_of(guess), rows_of(source), coefficient, leaf_map[0, 0], body_map[0, 0])
    return (own_map[None, None], own_out[None, None])


def solution(mesh):
    placed = (
        P("tx", "ty", None, None),
        P("tx", "ty", None, None),
        P("tx", "ty"),
        P("tx", "ty", None, None, None),
        P("tx", "ty", None, None, None),
    )
    return jax.shard_map(
        on_device,
        mesh=mesh,
        in_specs=placed,
        out_specs=(P("tx", "ty", None, None, None), P("tx", "ty", None, None, None)),
        check_vma=False,
    )
```

time: 103 us -> 59.3 us (0.58)
  other arithmetic: 23.4 us -> 0 us
  starting transfers between devices: 8.83 us -> 0 us
  local copies, waits for them, and re-layouts: 11.1 us -> 3.24 us
  Pallas kernels: 50.4 us -> 54.8 us
  matrix products: 4.16 us -> 0 us
  waiting for transfers between devices: 3.77 us -> 0 us
    sub x3 -> x0, other arithmetic: 11.3 us -> none  [the longest x1 11.3 us: residual_of(): diagonal_term * center[:, :, 0] + wave_term * DAMPING * center[:, :, 1]]
    ppermute x4 -> x0, starting transfers between devices: 8.83 us -> none  [the longest x2 6.25 us: padded_2(): lax.ppermute(tail, axis, [(i, (i + 1) % count) for i in range(ends)])]
    convert_element_type x2 -> x0, other arithmetic: 8.34 us -> none  [the longest x1 5.19 us: residual_of(): return (source.astype(jnp.float32) - applied).astype(jnp.bfloat16)]
    pallas_call x1, Pallas kernels: 50.4 us -> 54.8 us  [on_device(): pl.pallas_call(tree_kernel, name='build_tree', out_shape=(jax.ShapeDtypeS...]
    dot_general x1 -> x0, matrix products: 4.16 us -> none  [on_device(): jnp.einsum('ack,kbr->abcr', body_map[0, 0], cells, preferred_element_type...]
    reshape x1 -> x0, local copies, waits for them, and re-layouts: 3.96 us -> none  [on_device(): cells = residual.reshape(tile_len * tile_len, 2, guess.shape[3])]
    ppermute x4 -> x0, waiting for transfers between devices: 3.77 us -> none  [the longest x2 3.49 us: padded_2(): lax.ppermute(head, axis, [((i + 1) % count, i) for i in range(ends)])]
    add x1 -> x0, other arithmetic: 3.69 us -> none  [residual_of(): padded[2:, 1:-1] + padded[:-2, 1:-1] + padded[1:-1, 2:] + padded[1:-1, :-2]]
  transfers between devices with their start and end apart: 4 -> 0, of which waited for: 2 -> 0; matrix products, arithmetic and copies ran while one was open for 5% -> 0% of each run, Pallas kernels for 0% -> 0%
where the time goes in v1:
time: 59.3 us; the launch traced here: 58.7 us
  Pallas kernels  54.8 us (92%)
  local copies, waits for them, and re-layouts  3.24 us (5%)
  between operations  0.64 us (1%)
    pallas_call x1, Pallas kernels, on_device(): pl.pallas_call(tree_kernel, name='build_tree', out_shape=(jax.ShapeDtypeS...  54.8 us
    unnamed x2, local copies, waits for them, and re-layouts  3.24 us

profile of v1, /device:TPU:0, one launch (start us, length us, event | category | flops | bytes accessed | tf_op | source)
XLA Modules:
  0.0 58.7 jit_solution(13070480468025816683)
XLA Ops:
  0.6 54.8 %build_tree.1 = (f32[2,64,768]{2,1,0:T(8,128)}, f32[2,64,128]{2,1,0:T(8,128)}) custom-call(bf16[64,64,2,128]{3,2,1,0:T(2,128)(2,1)} %guess_ref.1, bf16[64,128,128]{2,1,0:T(8,128)(2,1)} %bitcast.6, bf16[64,128,128]{2,1,0:T(8,128)(2,1)} %bitcast.8, f32[64,64]{1,0:T(8,128)} %coef_ref.1, f32[2,256,256]{2,1,0:T(8,128)} %bitcast.9, bf16[2,256,4096]{2,1,0:T(8,128)(2,1)} %bitcast.7), custom_call_target="tpu_custom_call" | custom-call | tf_op jit(solution)/shard_map/build_tree/pallas_call | solution.py:484
  55.5 1.8 %copy.9 = f32[1,1,2,64,768]{4,3,2,1,0:T(8,128)} copy(f32[1,1,2,64,768]{4,3,2,1,0:T(8,128)} %bitcast.10) | data formatting | bytes 786432
  57.2 1.5 %copy.10 = f32[1,1,2,64,128]{4,3,2,1,0:T(8,128)} copy(f32[1,1,2,64,128]{4,3,2,1,0:T(8,128)} %bitcast.11) | data formatting | bytes 131072

commit v2 on v1

--- a/solution.py
+++ b/solution.py
@@ -13,7 +13,8 @@
 MESH = pl.DeviceIdType.MESH
 F32 = jnp.float32
 BF16 = jnp.bfloat16
-WIRE = F32
+WIRE = BF16
+UNROLL = 4
 
 
 def split(x):
@@ -182,70 +183,17 @@
     locals_[0].wait()
 
     def apart(k, carry):
-        plain[...] = guess_v[k].astype(F32)
+        slot = lax.rem(k, UNROLL)
+        plain[slot] = guess_v[k].astype(F32)
         for c in range(2):
-            field[c, k + 1, pad : pad + length] = plain[pl.ds(c, length, 2), :]
+            field[c, k + 1, pad : pad + length] = plain[slot, pl.ds(c, length, 2), :]
         return carry
 
-    lax.fori_loop(0, length, apart, 0)
+    lax.fori_loop(0, length, apart, 0, unroll=UNROLL)
     coef_v[...] = jnp.zeros_like(coef_v)
     coef_v[:length, :length] = coef_ref[...]
     coef_t = jnp.transpose(coef_v[...])[:length]
     coef_v[:length] = coef_t
-    for num, (exists, arrives, _, copy) in enumerate(halos):
-
-        @pl.when(arrives)
-        def _():
-            copy().wait_recv()
-            if num < 2:
-                plain[...] = edge_v[num].astype(F32)
-                for c in range(2):
-                    field[c, (0, length + 1)[num], pad : pad + length] = plain[pl.ds(c, length, 2), :]
-            else:
-                strip = beside_v[num - 2].astype(F32)
-                at = (pad - 1, pad + length)[num - 2]
-                for c in range(2):
-                    field[c, 1 : length + 1, at : at + 1] = strip[:, c : c + 1]
-
-        @pl.when(jnp.logical_not(arrives))
-        def _():
-            for c in range(2):
-                if num < 2:
-                    field[c, (0, length + 1)[num], pad : pad + length] = jnp.zeros((length, LANES), F32)
-                else:
-                    at = (pad - 1, pad + length)[num - 2]
-                    field[c, 1 : length + 1, at : at + 1] = jnp.zeros((length, 1, LANES), F32)
-
-    locals_[1].wait()
-
-    def residual_row(k, carry):
-        plain[...] = source_v[k].astype(F32)
-        wave_term = jnp.broadcast_to(
-            pltpu.roll(coef_v[:length], lax.rem(LANES - k, LANES), 1)[:, :1], (length, LANES)
-        )
-        diagonal_term = 4.0 - wave_term
-        damp = wave_term * DAMPING
-        center = [field[c, k + 1, pad : pad + length] for c in range(2)]
-        around = [
-            field[c, k + 2, pad : pad + length]
-            + field[c, k, pad : pad + length]
-            + field[c, k + 1, pad + 1 : pad + 1 + length]
-            + field[c, k + 1, pad - 1 : pad - 1 + length]
-            for c in range(2)
-        ]
-        real_part = diagonal_term * center[0] + damp * center[1] - around[0]
-        imag_part = diagonal_term * center[1] - damp * center[0] - around[1]
-        real = (plain[pl.ds(0, length, 2), :] - real_part).astype(BF16)
-        imag = (plain[pl.ds(1, length, 2), :] - imag_part).astype(BF16)
-        at = pl.ds(pl.multiple_of(k * length, length), length)
-        load_a[at, :LANES] = real
-        load_a[at, LANES:] = imag
-        load_b[at, :LANES] = -imag
-        load_b[at, LANES:] = real
-        return carry
-
-    lax.fori_loop(0, length, residual_row, 0)
-
     first.wait()
     mine = rows([m0[0, :side], m0[1, :side]])
     theirs = rows([face1[0], face1[1]])
@@ -284,6 +232,64 @@
     maps2[0].start()
     maps2[1].start()
 
+    for num, (exists, arrives, _, copy) in enumerate(halos):
+
+        @pl.when(arrives)
+        def _():
+            copy().wait_recv()
+            if num < 2:
+                plain[0] = edge_v[num].astype(F32)
+                for c in range(2):
+                    field[c, (0, length + 1)[num], pad : pad + length] = plain[0, pl.ds(c, length, 2), :]
+            else:
+                strip = beside_v[num - 2].astype(F32)
+                at = (pad - 1, pad + length)[num - 2]
+                for c in range(2):
+                    field[c, 1 : length + 1, at : at + 1] = strip[:, c : c + 1]
+
+        @pl.when(jnp.logical_not(arrives))
+        def _():
+            for c in range(2):
+                if num < 2:
+                    field[c, (0, length + 1)[num], pad : pad + length] = jnp.zeros((length, LANES), F32)
+                else:
+                    at = (pad - 1, pad + length)[num - 2]
+                    field[c, 1 : length + 1, at : at + 1] = jnp.zeros((length, 1, LANES), F32)
+
+    locals_[1].wait()
+
+    def residual_row(k, carry):
+        slot = lax.rem(k, UNROLL)
+        plain[slot] = source_v[k].astype(F32)
+        wave_term = jnp.broadcast_to(
+            pltpu.roll(coef_v[:length], lax.rem(LANES - k, LANES), 1)[:, :1], (length, LANES)
+        )
+        diagonal_term = 4.0 - wave_term
+        damp = wave_term * DAMPING
+        center = [field[c, k + 1, pad : pad + length] for c in range(2)]
+        around = [
+            field[c, k + 2, pad : pad + length]
+            + field[c, k, pad : pad + length]
+            + field[c, k + 1, pad + 1 : pad + 1 + length]
+            + field[c, k + 1, pad - 1 : pad - 1 + length]
+            for c in range(2)
+        ]
+        real_part = diagonal_term * center[0] + damp * center[1] - around[0]
+        imag_part = diagonal_term * center[1] - damp * center[0] - around[1]
+        real = (plain[slot, pl.ds(0, length, 2), :] - real_part).astype(BF16)
+        imag = (plain[slot, pl.ds(1, length, 2), :] - imag_part).astype(BF16)
+        at = pl.ds(pl.multiple_of(k * length, length), length)
+        load_a[at, :LANES] = real
+        load_a[at, LANES:] = imag
+        load_b[at, :LANES] = -imag
+        load_b[at, LANES:] = real
+        return carry
+
+    lax.fori_loop(0, length // 2, residual_row, 0, unroll=UNROLL)
+    maps2[0].wait_recv()
+    maps2[2].start()
+    lax.fori_loop(length // 2, length, residual_row, 0, unroll=UNROLL)
+
     locals_[2].wait()
     leaf = dot1(body_v[0], load_a[...]) + dot1(body_v[1], load_b[...])
     inv_ref[...] = leaf
@@ -294,8 +300,6 @@
             ]
     first_h = remote(h0.at[:, :side], face1h, send1.at[1], recv1.at[1], (vertical, q))
     first_h.start()
-    maps2[0].wait_recv()
-    maps2[2].start()
     first_h.wait()
     wave = dot3(
         cross1[1],
@@ -473,6 +477,11 @@
             copy().wait_send()
 
 
+def place_kernel(map_ref, out_ref, top_ref, top_out_ref):
+    top_ref[...] = map_ref[...]
+    top_out_ref[...] = out_ref[...]
+
+
 def on_device(source, guess, coefficient, leaf_map, body_map):
     length, width, _, rhs = guess.shape
     order = leaf_map.shape[3]
@@ -497,7 +506,7 @@
             pltpu.VMEM((2, 2 * width, rhs), BF16),
             pltpu.VMEM((2, length, 2, rhs), BF16),
             pltpu.VMEM((LANES, LANES), F32),
-            pltpu.VMEM((2 * width, rhs), F32),
+            pltpu.VMEM((UNROLL, 2 * width, rhs), F32),
             pltpu.VMEM((2, length + 2, width + 16, rhs), F32),
             pltpu.VMEM((length * width, 2 * rhs), BF16),
             pltpu.VMEM((length * width, 2 * rhs), BF16),
@@ -527,6 +536,16 @@
             collective_id=0, has_side_effects=True, vmem_limit_bytes=56 * 1024 * 1024
         ),
     )(guess, rows_of(guess), rows_of(source), coefficient, leaf_map[0, 0], body_map[0, 0])
+    own_map, own_out = pl.pallas_call(
+        place_kernel,
+        name="place",
+        out_shape=(
+            jax.ShapeDtypeStruct(own_map.shape, F32),
+            jax.ShapeDtypeStruct(own_out.shape, F32),
+        ),
+        in_specs=[vmem, vmem],
+        out_specs=(vmem, vmem),
+    )(own_map, own_out)
     return (own_map[None, None], own_out[None, None])
 
 

time: 59.3 us -> 46.3 us (0.78)
  Pallas kernels: 54.8 us -> 45.3 us
  local copies, waits for them, and re-layouts: 3.24 us -> 0 us
    pallas_call x1, Pallas kernels: 54.8 us -> 43.6 us  [on_device(): pl.pallas_call(tree_kernel, name='build_tree', out_shape=(jax.ShapeDtypeS...]
    unnamed x2 -> x0, local copies, waits for them, and re-layouts: 3.24 us -> none
    pallas_call x0 -> x1, Pallas kernels: none -> 1.78 us  [on_device(): pl.pallas_call(place_kernel, name='place', out_shape=(jax.ShapeDtypeStruc...]
where the time goes in v2:
time: 46.3 us; the launch traced here: 46 us
  Pallas kernels  45.3 us (98%)
  between operations  0.64 us (1%)
    pallas_call x1, Pallas kernels, on_device(): pl.pallas_call(tree_kernel, name='build_tree', out_shape=(jax.ShapeDtypeS...  43.6 us
    pallas_call x1, Pallas kernels, on_device(): pl.pallas_call(place_kernel, name='place', out_shape=(jax.ShapeDtypeStruc...  1.78 us

profile of v2, /device:TPU:0, one launch (start us, length us, event | category | flops | bytes accessed | tf_op | source)
XLA Modules:
  0.0 46.0 jit_solution(3680037063247836158)
XLA Ops:
  0.6 43.6 %build_tree.1 = (f32[2,64,768]{2,1,0:T(8,128)}, f32[2,64,128]{2,1,0:T(8,128)}) custom-call(bf16[64,64,2,128]{3,2,1,0:T(2,128)(2,1)} %guess_ref.1, bf16[64,128,128]{2,1,0:T(8,128)(2,1)} %bitcast.6, bf16[64,128,128]{2,1,0:T(8,128)(2,1)} %bitcast.8, f32[64,64]{1,0:T(8,128)} %coef_ref.1, f32[2,256,256]{2,1,0:T(8,128)} %bitcast.9, bf16[2,256,4096]{2,1,0:T(8,128)(2,1)} %bitcast.7), custom_call_target="tpu_custom_call" | custom-call | tf_op jit(solution)/shard_map/build_tree/pallas_call | solution.py:493
  44.2 1.8 %place.1 = (f32[2,64,768]{2,1,0:T(8,128)}, f32[2,64,128]{2,1,0:T(8,128)}) custom-call(f32[2,64,768]{2,1,0:T(8,128)} %get-tuple-element.6.map_ref, f32[2,64,128]{2,1,0:T(8,128)} %get-tuple-element.7.out_ref), custom_call_target="tpu_custom_call" | custom-call | tf_op jit(solution)/shard_map/place/pallas_call | solution.py:539

commit v3 on v2

--- a/solution.py
+++ b/solution.py
@@ -9,6 +9,7 @@
 
 DAMPING = 0.5
 DOUBLINGS = 7
+FINE = 2
 LANES = 128
 MESH = pl.DeviceIdType.MESH
 F32 = jnp.float32
@@ -76,19 +77,24 @@
 
 def inverse(power, pow_ref, inv_ref):
     n = power.shape[0]
-    pow_ref[:n, :n] = dot3(power, power)
-    inv_ref[:n, :n] = identity(n) + power
+    total = identity(n) + power
+    now = dot3(power, power)
+    for _ in range(FINE):
+        both = dot3(now, cols([now, total]))
+        now, total = both[:, :n], total + both[:, n:]
+    pow_ref[:n, :n] = now.astype(BF16)
+    inv_ref[:n, :n] = total
 
     def body(k, carry):
         now, total = pow_ref[:n, :n], inv_ref[:n, :n]
-        both = dot3(now, cols([now, total]))
-        pow_ref[:n, :n] = both[:, :n]
+        both = dot1(now, cols([now, total.astype(BF16)]))
+        pow_ref[:n, :n] = both[:, :n].astype(BF16)
         inv_ref[:n, :n] = total + both[:, n:]
         return carry
 
-    lax.fori_loop(0, DOUBLINGS - 2, body, 0)
+    lax.fori_loop(0, DOUBLINGS - 2 - FINE, body, 0)
     total = inv_ref[:n, :n]
-    return total + dot3(pow_ref[:n, :n], total)
+    return total + dot1(pow_ref[:n, :n], total.astype(BF16))
 
 
 def swapped_view(block):
@@ -96,9 +102,9 @@
 
 
 def tree_kernel(
-    guess_ref, guess_rows_ref, source_ref, coef_ref, map_ref, body_ref, top_ref, top_out_ref,
-    guess_v, source_v, body_v, edge_v, beside_v, coef_v, plain, field, load_a, load_b,
-    m0, h0, m1, h1, m2, h2, out2, out3,
+    guess_ref, guess_rows_ref, source_ref, coef_hbm, map_hbm, body_ref, top_ref, top_out_ref,
+    guess_v, source_v, body_v, coef_ref, map_ref, edge_v, beside_v, coef_v, plain, field, load_a, load_b,
+    m0, h0, m1, h1, m2, h2, out1, out2, out3,
     face1, face1h, face2, face2h, face3, face3h, pow_ref, inv_ref, cross1, cross2, cross3,
     local_sem, halo_send, halo_recv, send1, recv1, send2, recv2, send3, recv3,
 ):
@@ -135,6 +141,12 @@
         (q > 0, q < q_ends, (p, q - 1),
          lambda: remote(guess_ref.at[:, 0], beside_v.at[1], halo_send.at[3], halo_recv.at[3], (p, q - 1))),
     ]
+    early = [
+        pltpu.make_async_copy(map_hbm, map_ref, local_sem.at[3]),
+        pltpu.make_async_copy(coef_hbm, coef_ref, local_sem.at[4]),
+    ]
+    for copy in early:
+        copy.start()
     locals_ = [
         pltpu.make_async_copy(guess_rows_ref, guess_v, local_sem.at[0]),
         pltpu.make_async_copy(source_ref, source_v, local_sem.at[1]),
@@ -169,7 +181,9 @@
     vert_swap = jnp.where(p_odd == 1, 0, 1)
     cross = jnp.where(lane < LANES // 2, vert_swap, q_odd) == 1
 
-    first = remote(m0.at[:, :side], face1, send1.at[0], recv1.at[0], (vertical, q))
+    for copy in early:
+        copy.wait()
+    first = remote(out1, face1, send1.at[0], recv1.at[0], (vertical, q))
     for k in range(4):
         for c in range(2):
             left = map_ref[c, pl.ds(starts[k], side), :LANES]
@@ -177,6 +191,7 @@
             m0[c, k * side : (k + 1) * side, :LANES] = jnp.where(cross, right, left)
             m0[c, k * side : (k + 1) * side, LANES:] = jnp.where(cross, left, right)
         if k == 0:
+            out1[...] = m0[:, :side].astype(WIRE)
             first.start()
 
     pad = 8
@@ -196,7 +211,7 @@
     coef_v[:length] = coef_t
     first.wait()
     mine = rows([m0[0, :side], m0[1, :side]])
-    theirs = rows([face1[0], face1[1]])
+    theirs = rows([face1[0].astype(F32), face1[1].astype(F32)])
     across = embed_low(theirs[:side, :LANES], theirs[side:, :LANES])
     cross1[0] = across
     product = dot3(across, mine)
@@ -362,18 +377,28 @@
     out3[...] = m2[:, :side].astype(WIRE)
 
     def last_copies(src, face, kind):
+        first_rows = src
         def send(source, box, slot, target):
             return remote(
                 source, face.at[box, q_odd], send3.at[kind, slot], recv3.at[kind, slot], target
             )
 
+        def plane(source, slot, target):
+            return [
+                lambda c=c: remote(
+                    source(c), face.at[1, q_odd, c],
+                    send3.at[kind, slot + c], recv3.at[kind, slot + c], target,
+                )
+                for c in range(2)
+            ]
+
         return (
             lambda: send(src, 0, 0, (vertical, q)),
-            lambda: send(face.at[1, q_odd], 1, 1, (vertical, q)),
-            lambda: send(src, 1, 2, (facing, q)),
-            lambda: send(src, 0, 3, (p, beside)),
-            lambda: send(face.at[0, q_odd], 0, 3, (p, beside)),
-            lambda: send(face.at[1, q_odd], 1, 4, (p, beside)),
+            plane(lambda c: face.at[1, q_odd, c], 2, (vertical, q)),
+            plane(lambda c: first_rows.at[c], 4, (facing, q)),
+            lambda: send(src, 0, 1, (p, beside)),
+            lambda: send(face.at[0, q_odd], 0, 1, (p, beside)),
+            plane(lambda c: face.at[1, q_odd, c], 6, (p, beside)),
         )
 
     def last_start(copies, src, face):
@@ -381,42 +406,51 @@
 
         @pl.when(inner)
         def _():
-            over().start()
+            for c in range(2):
+                over[c]().start()
             up_own().start()
             side_own().start()
             face[0, q_odd] = src[:, :side]
 
-    def last_relay(copies):
+    def inner_relay(copies):
         up_own, up_other, over, side_own, side_relay, side_other = copies
 
         @pl.when(inner)
         def _():
-            over().wait_recv()
-            up_other().start()
-            side_other().start()
+            for c in range(2):
+                over[c]().wait_recv()
+                up_other[c]().start()
+                side_other[c]().start()
+
+    def outer_relay(copies):
+        up_own, up_other, over, side_own, side_relay, side_other = copies
 
         @pl.when(jnp.logical_not(inner))
         def _():
             up_own().wait_recv()
             side_relay().start()
-            up_other().wait_recv()
-            side_other().start()
+            for c in range(2):
+                up_other[c]().wait_recv()
+                side_other[c]().start()
 
     def last_wait(copies):
         up_own, up_other, over, side_own, side_relay, side_other = copies
         side_own().wait_recv()
-        side_other().wait_recv()
+        for c in range(2):
+            side_other[c]().wait_recv()
 
     def last_drain(copies):
         up_own, up_other, over, side_own, side_relay, side_other = copies
         side_own().wait_send()
-        side_other().wait_send()
+        for c in range(2):
+            side_other[c]().wait_send()
 
         @pl.when(inner)
         def _():
-            over().wait_send()
             up_own().wait_send()
-            up_other().wait_send()
+            for c in range(2):
+                over[c]().wait_send()
+                up_other[c]().wait_send()
 
     maps3 = last_copies(out3, face3, 0)
     last_start(maps3, out3, face3)
@@ -434,8 +468,9 @@
         h2[c] = gain[c * count2 : (c + 1) * count2] + h1[c, side:]
     data3 = last_copies(h2.at[:, :side], face3h, 1)
     last_start(data3, h2, face3h)
-    last_relay(maps3)
-    last_relay(data3)
+    inner_relay(maps3)
+    outer_relay(maps3)
+    inner_relay(data3)
 
     last_wait(maps3)
     mine = rows([face3[0, j, c].astype(F32) for c in range(2) for j in range(2)])
@@ -460,6 +495,7 @@
         up = [jnp.where(lower, b, a) for a, b in zip(own, other)]
         for k, value in enumerate([low[0], low[1], low[2], up[1], up[0], up[2]]):
             top_ref[c, :, k * LANES : (k + 1) * LANES] = value
+    outer_relay(data3)
     last_wait(data3)
     mine = rows([face3h[0, j, c] for c in range(2) for j in range(2)])
     theirs = rows([face3h[1, j, c] for c in range(2) for j in range(2)])
@@ -497,12 +533,14 @@
             jax.ShapeDtypeStruct((2, side, 12 * side), F32),
             jax.ShapeDtypeStruct((2, side, rhs), F32),
         ),
-        in_specs=[hbm, hbm, hbm, vmem, vmem, hbm],
+        in_specs=[hbm] * 6,
         out_specs=(vmem, vmem),
         scratch_shapes=[
             pltpu.VMEM((length, 2 * width, rhs), BF16),
             pltpu.VMEM((length, 2 * width, rhs), BF16),
             pltpu.VMEM((2, order, length * width), BF16),
+            pltpu.VMEM((length, width), F32),
+            pltpu.VMEM((2, order, order), F32),
             pltpu.VMEM((2, 2 * width, rhs), BF16),
             pltpu.VMEM((2, length, 2, rhs), BF16),
             pltpu.VMEM((LANES, LANES), F32),
@@ -516,21 +554,22 @@
             pltpu.VMEM((2, 3 * side, rhs), F32),
             pltpu.VMEM((2, 2 * side, 8 * side), F32),
             pltpu.VMEM((2, 2 * side, rhs), F32),
+            pltpu.VMEM((2, side, order), WIRE),
             pltpu.VMEM((2, side, 6 * side), WIRE),
             pltpu.VMEM((2, side, 8 * side), WIRE),
-            pltpu.VMEM((2, side, order), F32),
+            pltpu.VMEM((2, side, order), WIRE),
             pltpu.VMEM((2, side, rhs), F32),
             pltpu.VMEM((3, 2, side, 6 * side), WIRE),
             pltpu.VMEM((3, 2, side, rhs), F32),
             pltpu.VMEM((2, 2, 2, side, 8 * side), WIRE),
             pltpu.VMEM((2, 2, 2, side, rhs), F32),
-            pltpu.VMEM((order, order), F32),
+            pltpu.VMEM((order, order), BF16),
             pltpu.VMEM((order, order), F32),
             pltpu.VMEM((2, 2 * side, 2 * side), F32),
             pltpu.VMEM((2, order, order), F32),
             pltpu.VMEM((2, order, order), F32),
-            dma((3,)), dma((4,)), dma((4,)), dma((2,)), dma((2,)),
-            dma((2, 3)), dma((2, 3)), dma((2, 5)), dma((2, 5)),
+            dma((5,)), dma((4,)), dma((4,)), dma((2,)), dma((2,)),
+            dma((2, 3)), dma((2, 3)), dma((2, 8)), dma((2, 8)),
         ],
         compiler_params=pltpu.CompilerParams(
             collective_id=0, has_side_effects=True, vmem_limit_bytes=56 * 1024 * 1024

time: 46.3 us -> 43.4 us (0.937)
  Pallas kernels: 45.3 us -> 42.6 us
    pallas_call x1, Pallas kernels: 43.6 us -> 40.8 us  [on_device(): pl.pallas_call(tree_kernel, name='build_tree', out_shape=(jax.ShapeDtypeS...]
where the time goes in v3:
time: 43.4 us; the launch traced here: 43.3 us
  Pallas kernels  42.6 us (98%)
  between operations  0.64 us (1%)
    pallas_call x1, Pallas kernels, on_device(): pl.pallas_call(tree_kernel, name='build_tree', out_shape=(jax.ShapeDtypeS...  40.8 us
    pallas_call x1, Pallas kernels, on_device(): pl.pallas_call(place_kernel, name='place', out_shape=(jax.ShapeDtypeStruc...  1.78 us

profile of v3, /device:TPU:0, one launch (start us, length us, event | category | flops | bytes accessed | tf_op | source)
XLA Modules:
  0.0 43.3 jit_solution(14152213149797789847)
XLA Ops:
  0.6 40.8 %build_tree.1 = (f32[2,64,768]{2,1,0:T(8,128)}, f32[2,64,128]{2,1,0:T(8,128)}) custom-call(bf16[64,64,2,128]{3,2,1,0:T(2,128)(2,1)} %guess_ref.1, bf16[64,128,128]{2,1,0:T(8,128)(2,1)} %bitcast.6, bf16[64,128,128]{2,1,0:T(8,128)(2,1)} %bitcast.8, f32[64,64]{1,0:T(8,128)} %coef_hbm.1, f32[2,256,256]{2,1,0:T(8,128)} %bitcast.9, bf16[2,256,4096]{2,1,0:T(8,128)(2,1)} %bitcast.7), custom_call_target="tpu_custom_call" | custom-call | tf_op jit(solution)/shard_map/build_tree/pallas_call | solution.py:529
  41.5 1.8 %place.1 = (f32[2,64,768]{2,1,0:T(8,128)}, f32[2,64,128]{2,1,0:T(8,128)}) custom-call(f32[2,64,768]{2,1,0:T(8,128)} %get-tuple-element.6.map_ref, f32[2,64,128]{2,1,0:T(8,128)} %get-tuple-element.7.out_ref), custom_call_target="tpu_custom_call" | custom-call | tf_op jit(solution)/shard_map/place/pallas_call | solution.py:578

commit v4 on v3

--- a/solution.py
+++ b/solution.py
@@ -31,6 +31,10 @@
     a_high, a_low = split(a)
     b_high, b_low = split(b)
     return dot1(a_high, b_high) + (dot1(a_high, b_low) + dot1(a_low, b_high))
+
+
+def dotw(a, b):
+    return dot1(a.astype(BF16), b.astype(BF16))
 
 
 def tile(x, k):
@@ -164,12 +168,6 @@
             pl.semaphore_signal(barrier, inc=1, device_id=target, device_id_type=MESH)
 
     pl.semaphore_wait(barrier, arrivals)
-    for exists, _, _, copy in halos:
-
-        @pl.when(exists)
-        def _():
-            copy().start()
-
     starts = [
         jnp.where(p_odd == 1, 0, 2 * side),
         jnp.where(q_odd == 1, 3 * side, side),
@@ -193,6 +191,12 @@
         if k == 0:
             out1[...] = m0[:, :side].astype(WIRE)
             first.start()
+
+    for exists, _, _, copy in halos:
+
+        @pl.when(exists)
+        def _():
+            copy().start()
 
     pad = 8
     locals_[0].wait()
@@ -476,15 +480,15 @@
     mine = rows([face3[0, j, c].astype(F32) for c in range(2) for j in range(2)])
     theirs = rows([face3[1, j, c].astype(F32) for c in range(2) for j in range(2)])
     across = embed(theirs[: 2 * side, :LANES], theirs[2 * side :, :LANES])
-    product = dot3(across, mine)
+    product = dotw(across, mine)
     turned = tile(product, 0)
     inv = inverse(embed(turned[: 2 * side], turned[2 * side :]), pow_ref, inv_ref)
     begin = pl.multiple_of(inner_num * side, side)
     rest = m2[0, pl.ds(begin, side)], m2[1, pl.ds(begin, side)]
-    out_gain = dot3(embed(tile(rest[0], 0), tile(rest[1], 0)), inv)
+    out_gain = dotw(embed(tile(rest[0], 0), tile(rest[1], 0)), inv)
     cross3[0] = across
     cross3[1, : 2 * side] = out_gain
-    gain = dot3(out_gain, cols(
+    gain = dotw(out_gain, cols(
         [tile(product, k) for k in range(1, 4)] + [-tile(theirs, k) for k in range(1, 4)]
     ))
     for c in range(2):

time: 43.4 us -> 42.8 us (0.986)
  Pallas kernels: 42.6 us -> 42 us
    pallas_call x1, Pallas kernels: 40.8 us -> 40.2 us  [on_device(): pl.pallas_call(tree_kernel, name='build_tree', out_shape=(jax.ShapeDtypeS...]
where the time goes in v4:
time: 42.8 us; the launch traced here: 42.7 us
  Pallas kernels  42 us (98%)
  between operations  0.64 us (1%)
    pallas_call x1, Pallas kernels, on_device(): pl.pallas_call(tree_kernel, name='build_tree', out_shape=(jax.ShapeDtypeS...  40.2 us
    pallas_call x1, Pallas kernels, on_device(): pl.pallas_call(place_kernel, name='place', out_shape=(jax.ShapeDtypeStruc...  1.78 us

profile of v4, /device:TPU:0, one launch (start us, length us, event | category | flops | bytes accessed | tf_op | source)
XLA Modules:
  0.0 42.7 jit_solution(6257999782400146169)
XLA Ops:
  0.6 40.2 %build_tree.1 = (f32[2,64,768]{2,1,0:T(8,128)}, f32[2,64,128]{2,1,0:T(8,128)}) custom-call(bf16[64,64,2,128]{3,2,1,0:T(2,128)(2,1)} %guess_ref.1, bf16[64,128,128]{2,1,0:T(8,128)(2,1)} %bitcast.6, bf16[64,128,128]{2,1,0:T(8,128)(2,1)} %bitcast.8, f32[64,64]{1,0:T(8,128)} %coef_hbm.1, f32[2,256,256]{2,1,0:T(8,128)} %bitcast.9, bf16[2,256,4096]{2,1,0:T(8,128)(2,1)} %bitcast.7), custom_call_target="tpu_custom_call" | custom-call | tf_op jit(solution)/shard_map/build_tree/pallas_call | solution.py:533
  40.9 1.8 %place.1 = (f32[2,64,768]{2,1,0:T(8,128)}, f32[2,64,128]{2,1,0:T(8,128)}) custom-call(f32[2,64,768]{2,1,0:T(8,128)} %get-tuple-element.6.map_ref, f32[2,64,128]{2,1,0:T(8,128)} %get-tuple-element.7.out_ref), custom_call_target="tpu_custom_call" | custom-call | tf_op jit(solution)/shard_map/place/pallas_call | solution.py:582
